TPU v7x, 32 devices: a whole 2x2x4 slice. The times are simulated.
32 devices in a mesh: row: 4 (over x, core), col: 8 (over z, y).
Axes of the slice: x: 2, y: 2, z: 4, core: 2. Of those that a mesh axis runs over, the one named last changes fastest.
Arguments:
- node_features: bfloat16 [4096, 256], P(('row', 'col')), may hold values from -6 to 6
- layer_weight: bfloat16 [256, 256], replicated, may hold values from -0.375 to 0.375
- output_grad: bfloat16 [4096, 256], P(('row', 'col')), may hold values from -6 to 6
- block_values: bfloat16 [4, 8, 24, 128, 128], P('row', 'col'), may hold values from -0.15625 to 0.15625
- block_position: int32 [4, 8, 24], P('row', 'col'), may hold values from 0 to 31, as said below
- tile_count: int32 [4, 8], P('row', 'col'), may hold values from 6 to 24, as said below
Outputs:
- node_output: bfloat16 [4096, 256], P(('row', 'col'))
- input_grad: bfloat16 [4096, 256], P(('row', 'col'))
- weight_grad: float32 [256, 256], replicated
Inputs may be any that keep to these rules, and one draw needn't show every extreme that they name: Tile (r, c) uses its slots 0 to tile_count[r, c] - 1; in every draw some tile uses all 24 slots. `block_position`: the slots of a tile hold distinct positions in increasing order.
All inputs are finite; a program needn't handle non-finite values.
Results may differ from a plain program's by a relative error of at most 0.02.
Values may be sent and summed in bfloat16 or wider, within the bound.
A program may use at most 64 MiB of HBM per device.

v0:
```python
import math

import jax
import jax.numpy as jnp
from jax import lax
from jax.sharding import PartitionSpec as P


def elu_slope(pre_activation):
    return jnp.where(pre_activation > 0, 1.0, jnp.exp(jnp.minimum(pre_activation, 0.0)))


def tile_product(
    values, source_block, target_block, live_count, panel_rows, target_count, transposed
):
    slot_total = values.shape[0]
    block = values.shape[1]
    width = panel_rows.shape[1]
    panel_blocks = panel_rows.reshape(-1, block, width)
    group_size = math.gcd(slot_total, 32)
    group_count = (live_count + group_size - 1) // group_size

    def add_group(number, running):
        first_slot = number * group_size
        group_values = lax.dynamic_slice_in_dim(values, first_slot, group_size, 0)
        group_source = lax.dynamic_slice_in_dim(source_block, first_slot, group_size, 0)
        group_target = lax.dynamic_slice_in_dim(target_block, first_slot, group_size, 0)
        slot_index = first_slot + jnp.arange(group_size, dtype=jnp.int32)
        picked = jnp.take(panel_blocks, group_source, axis=0)
        if transposed:
            product = jnp.einsum(
                "nij,nif->njf", group_values, picked, preferred_element_type=jnp.float32
            )
        else:
            product = jnp.einsum(
                "nij,njf->nif", group_values, picked, preferred_element_type=jnp.float32
            )
        live = (slot_index < live_count).astype(jnp.float32)
        return running.at[group_target].add(product * live[:, None, None])

    running = lax.fori_loop(
        0, group_count, add_group, jnp.zeros((target_count, block, width), jnp.float32)
    )
    return running.reshape(target_count * block, width)


def body(node_features, layer_weight, output_grad, block_values, block_position, tile_count):
    values = block_values[0, 0]
    position = block_position[0, 0]
    live_count = tile_count[0, 0]
    node_dev = node_features.shape[0]
    block = values.shape[1]
    row_blocks = lax.axis_size("col") * node_dev // block
    col_blocks = lax.axis_size("row") * node_dev // block
    block_row = position // col_blocks
    block_col = position % col_blocks
    grad_scale = 1.0 / math.sqrt(node_dev * lax.axis_size("row") * lax.axis_size("col"))
    projected = jnp.dot(node_features, layer_weight, preferred_element_type=jnp.float32).astype(
        jnp.bfloat16
    )
    col_panel = lax.all_gather(projected, "row", axis=0, tiled=True)
    partial_rows = tile_product(
        values, block_col, block_row, live_count, col_panel, row_blocks, False
    )
    summed = lax.psum(partial_rows.astype(jnp.bfloat16), "col").astype(jnp.float32)
    own_first = lax.axis_index("col") * node_dev
    own_sum = lax.dynamic_slice_in_dim(summed, own_first, node_dev, 0)
    grad_panel = lax.all_gather(output_grad, "col", axis=0, tiled=True)
    row_panel = (grad_panel.astype(jnp.float32) * elu_slope(summed)).astype(jnp.bfloat16)
    node_output = jax.nn.elu(own_sum).astype(jnp.bfloat16)
    partial_cols = tile_product(
        values, block_row, block_col, live_count, row_panel, col_blocks, True
    )
    column_grad = lax.psum_scatter(
        partial_cols.astype(jnp.bfloat16), "row", scatter_dimension=0, tiled=True
    ).astype(jnp.float32)
    input_grad = jnp.einsum(
        "nf,gf->ng", column_grad, layer_weight.astype(jnp.float32), precision=lax.Precision.HIGHEST
    ).astype(jnp.bfloat16)
    weight_term = (
        jnp.einsum(
            "nf,ng->fg",
            node_features.astype(jnp.float32),
            column_grad,
            precision=lax.Precision.HIGHEST,
        )
        * grad_scale
    )
    weight_grad = lax.psum(weight_term, ("row", "col"))
    return (node_output, input_grad, weight_grad)


def solution(mesh):
    in_specs = (
        P(("row", "col"), None),
        P(),
        P(("row", "col"), None),
        P("row", "col", None, None, None),
        P("row", "col", None),
        P("row", "col"),
    )
    out_specs = (P(("row", "col"), None), P(("row", "col"), None), P())
    return jax.shard_map(body, mesh=mesh, in_specs=in_specs, out_specs=out_specs, check_vma=False)
```

profile of v0, /device:TPU:0, one launch (start us, length us, event | category | flops | bytes accessed | tf_op | source)
XLA Modules:
  0.0 278.4 jit_solution(15982692852787990856)
XLA Ops:
  7.2 0.0 copy-start
  7.2 0.0 all-reduce.3.cloned.1.call-start
  7.9 0.0 copy-start.6
  7.9 0.6 copy-done.6
  8.6 0.0 copy-done
  8.6 1.0 convolution_convert_fusion.1
  9.6 7.2 %all_gather.6 = bf16[512,256]{1,0:T(8,128)(2,1)S(1)} all-gather(bf16[128,256]{1,0:T(8,128)(2,1)S(1)} %convolution_convert_fusion.1), channel_id=1, replica_groups=mesh['row'=4,'col'=8] {'row'}, dimensions={0}, use_global_device_ids=true | all-gather | bytes 327680 | tf_op jit(solution)/shard_map/all_gather | solution.py:61
  16.8 0.1 broadcast_in_dim.45
  16.9 4.1 %while.20 = (s32[]{:T(128)}, f32[8,128,256]{2,1,0:T(8,128)S(1)}, s32[]{:T(128)}, s32[24]{0:T(128)S(1)}, bf16[24,128,128]{2,1,0:T(8,128)(2,1)}, /*index=5*/s32[24...) while((s32[]{:T(128)}, f32[8,128,256]{2,1,0:T(8,128)S(1)}, ...), condition=%wide.region_2.3_spmd, body=%wide.region_0.2_spmd.sunk | while | flops 67896424 | bytes 6033903 | solution.py:41
  16.9 0.1 compare_select_fusion.13
  17.0 0.7 compare_and_fusion.4
  17.7 0.6 gather_fusion
  18.3 1.3 convolution_multiply_fusion.5
  19.7 1.3 scatter_fusion
  21.0 0.0 copy-start.1
  21.0 0.9 convert_element_type.48
  21.9 0.0 all-reduce.3.cloned.1.call-update
  21.9 0.0 reduce-scatter.2.cloned.1.call-start
  21.9 0.4 copy-done.1
  22.3 0.0 copy-start.5
  22.3 0.4 copy.9
  22.7 0.5 copy-done.5
  23.2 38.4 %all_gather.7 = bf16[1024,256]{1,0:T(8,128)(2,1)S(1)} all-gather(bf16[128,256]{1,0:T(8,128)(2,1)S(1)} %copy-done.5), channel_id=1, replica_groups=mesh['row'=4,'col'=8] {'col'}, dimensions={0}, use_global_device_ids=true | all-gather | bytes 589824 | tf_op jit(solution)/shard_map/all_gather | solution.py:68
  61.6 43.1 %all-reduce.3.cloned.1.call-done = bf16[1024,256]{1,0:T(8,128)(2,1)} async-done(((bf16[1024,256]{1,0:T(8,128)(2,1)}), bf16[1024,256]{1,0:T(8,128)(2,1)}) %all-reduce.3.cloned.1.call-update) | async-done | bytes 524304 | tf_op jit(solution)/shard_map/psum | solution.py:65
  104.7 1.3 multiply_convert_fusion
  106.0 3.8 %while.21 = (s32[]{:T(128)}, f32[4,128,256]{2,1,0:T(8,128)S(1)}, s32[]{:T(128)}, s32[24]{0:T(128)S(1)}, bf16[24,128,128]{1,2,0:T(8,128)(2,1)S(1)}, /*index=5*/s3...) while((s32[]{:T(128)}, f32[4,128,256]{2,1,0:T(8,128)S(1)}, ...), condition=%wide.region_6.7_spmd, body=%wide.region_4.6_spmd.sunk | while | flops 67896424 | bytes 6034887 | solution.py:41
  106.1 0.6 compare_select_fusion.14
  106.7 0.7 compare_and_fusion.5
  107.4 0.6 gather_fusion.1
  108.0 0.4 convolution_multiply_fusion.6
  108.4 1.4 scatter_fusion.1
  109.8 0.0 copy-start.2
  109.8 0.7 convert_element_type.54
  110.6 0.0 reduce-scatter.2.cloned.1.call-update
  110.6 0.0 all-reduce.5.cloned.1.call-start
  110.6 0.3 copy-done.2
  110.9 0.1 convert_element_type.50
  111.0 0.0 copy-start.3
  111.0 0.7 fusion.14
  111.7 25.7 %reduce-scatter.2.cloned.1.call-done = bf16[128,256]{1,0:T(8,128)(2,1)} async-done(((bf16[512,256]{1,0:T(8,128)(2,1)}), bf16[128,256]{1,0:T(8,128)(2,1)}) %reduce-scatter.2.cloned.1.call-update) | async-done | bytes 65552 | tf_op jit(solution)/shard_map/reduce_scatter | solution.py:74
  137.4 0.0 copy-done.3
  137.4 1.8 fusion.12
  139.2 0.0 copy-start.4
  139.2 0.0 all-reduce.5.cloned.1.call-update
  139.2 0.8 copy-done.4
  140.0 0.8 convolution_convert_fusion
  140.8 129.3 %all-reduce.5.cloned.1.call-done = f32[256,256]{0,1:T(8,128)} async-done(((f32[256,256]{0,1:T(8,128)}), f32[256,256]{0,1:T(8,128)}) %all-reduce.5.cloned.1.call-update) | async-done | bytes 262160 | tf_op jit(solution)/shard_map/psum | solution.py:89
  270.1 1.8 copy.11
  (4 shorter events, 0.1 us)
Async XLA Ops:
  7.2 1.4 copy-start
  7.2 97.5 %all-reduce.3.cloned.1.call-start = ((), (), s32[]{:S(2)}) async-start(), calls=%async_computation.1 | async-start | bytes 1048576 | tf_op jit(solution)/shard_map/psum | solution.py:65
  7.9 0.7 copy-start.6
  21.0 1.3 copy-start.1
  21.9 115.5 %reduce-scatter.2.cloned.1.call-start = ((), (), s32[]{:S(2)}) async-start(), calls=%async_computation.2 | async-start | bytes 327680 | tf_op jit(solution)/shard_map/reduce_scatter | solution.py:74
  22.3 0.8 copy-start.5
  109.8 1.1 copy-start.2
  110.6 159.5 %all-reduce.5.cloned.1.call-start = ((), (), s32[]{:S(2)}) async-start(), calls=%async_computation.3 | async-start | bytes 524288 | tf_op jit(solution)/shard_map/psum | solution.py:89
  111.0 26.4 %copy-start.3 = (bf16[128,256]{1,0:T(8,128)(2,1)S(1)}, bf16[128,256]{1,0:T(8,128)(2,1)}, u32[]{:S(2)}) copy-start(bf16[128,256]{1,0:T(8,128)(2,1)} %param.10) | copy-start | bytes 196612
  139.2 0.8 copy-start.4
Sparse Core Ops, SparseCore 0:
  22.0 82.5 all-reduce.2
  110.7 26.6 reduce-scatter.1
  143.5 126.5 all-reduce.4
where the time goes:
time: 278 us
  waiting for transfers between devices  198 us (71%)
  blocking collectives  45.6 us (16%)
  between operations  14.6 us (5%)
  other arithmetic  8.59 us (3%)
  local copies, waits for them, and re-layouts  6.08 us (2%)
  matrix products  5.27 us (2%)
    psum x1, waiting for transfers between devices, body(): weight_grad = lax.psum(weight_term, ('row', 'col'))  129 us
    psum x1, waiting for transfers between devices, body(): lax.psum(partial_rows.astype(jnp.bfloat16), 'col').astype(jnp.float32)  43.1 us
    all_gather x1, blocking collectives, body(): grad_panel = lax.all_gather(output_grad, 'col', axis=0, tiled=True)  38.4 us
    reduce_scatter x1, waiting for transfers between devices, body(): lax.psum_scatter(partial_cols.astype(jnp.bfloat16), 'row', scatter_dimens...  25.7 us
    all_gather x1, blocking collectives, body(): col_panel = lax.all_gather(projected, 'row', axis=0, tiled=True)  7.22 us
  transfers between devices with their start and end apart: 3, of which 3 were waited for; matrix products, arithmetic and copies ran while one was open for 1% of the time, Pallas kernels for 0%

commit v1 on v0

v1 whole, which is shorter than its diff:
```python
import functools
import math

import jax
import jax.numpy as jnp
from jax import lax
from jax.experimental import pallas as pl
from jax.experimental.pallas import tpu as pltpu
from jax.sharding import PartitionSpec as P

MESH = pl.DeviceIdType.MESH
F32 = jnp.float32
BF16 = jnp.bfloat16


def repeat(start, stop, step):
    if stop - start <= 8:
        for d in range(start, stop):
            step(d)
    else:

        def one(d, unused):
            step(d)
            return unused

        lax.fori_loop(start, stop, one, 0)


def split_dot(left, right, dims):
    high = left.astype(BF16)
    low = (left - high.astype(F32)).astype(BF16)
    first = lax.dot_general(high, right, dims, preferred_element_type=F32)
    return first + lax.dot_general(low, right, dims, preferred_element_type=F32)


def kernel(
    rows,
    cols,
    position,
    count,
    x_ref,
    w_ref,
    og_ref,
    values_hbm,
    out_ref,
    ig_ref,
    wg_ref,
    values,
    xg,
    tile,
    tile_t,
    part,
    part_in,
    up,
    acc,
    pc,
    pc_in,
    term,
    w1_in,
    own,
    w2_in,
    small,
    w3_in,
    w4_in,
    sem_v,
    sem_x,
    sem_p,
    sem_u,
    sem_c,
    sem_w1,
    sem_w2,
    sem_w3,
    sem_w4,
):
    nodes, width = x_ref.shape
    slots, block = values_hbm.shape[0], values_hbm.shape[1]
    col_blocks = rows
    my_row = lax.axis_index("row")
    my_col = lax.axis_index("col")
    size = {"row": rows, "col": cols}
    me = {"row": my_row, "col": my_col}

    def ahead(axis, d):
        return lax.rem(me[axis] + d, size[axis])

    def behind(axis, d):
        return lax.rem(me[axis] + size[axis] - d, size[axis])

    def send(axis, sem, d, src, dst):
        return pltpu.make_async_remote_copy(
            src_ref=src,
            dst_ref=dst,
            send_sem=sem.at[0, d - 1],
            recv_sem=sem.at[1, d - 1],
            device_id={axis: ahead(axis, d)},
            device_id_type=MESH,
        )

    load = pltpu.make_async_copy(values_hbm, values.at[pl.ds(0, slots)], sem_v)
    load.start()

    barrier = pltpu.get_barrier_semaphore()
    for axis in ("row", "col"):

        def greet(d, axis=axis):
            pl.semaphore_signal(
                barrier, inc=1, device_id={axis: ahead(axis, d)}, device_id_type=MESH
            )

        repeat(1, size[axis], greet)
    pl.semaphore_wait(barrier, rows + cols - 2)

    repeat(1, rows, lambda d: send("row", sem_x, d, x_ref, xg.at[my_row]).start())
    xg[my_row] = x_ref[...]

    values[slots] = jnp.zeros((block, block), BF16)
    load.wait()
    live_count = count[0]

    def build(q, pointer):
        for k in range(col_blocks):
            here = position[jnp.minimum(pointer, slots - 1)]
            live = (here == q * col_blocks + k) & (pointer < live_count)
            slot = jnp.where(live, pointer, slots)
            tile[q, :, pl.ds(k * block, block)] = values[slot]
            pointer = pointer + live.astype(jnp.int32)
        return pointer

    if cols <= 8:
        pointer = jnp.int32(0)
        for q in range(cols):
            pointer = build(q, pointer)
    else:
        lax.fori_loop(0, cols, build, jnp.int32(0))

    def from_row(d):
        slot = xg.at[behind("row", d)]
        send("row", sem_x, d, slot, slot).wait_recv()

    repeat(1, rows, from_row)
    panel = xg[...].reshape(rows * nodes, width)

    def forward(d):
        to = ahead("col", d)
        product = jnp.dot(tile[to], panel, preferred_element_type=F32)
        part[to] = product.astype(BF16)
        send("col", sem_p, d, part.at[to], part_in.at[my_col]).start()

    repeat(1, cols, forward)
    small_sum = jnp.dot(tile[my_col], panel, preferred_element_type=F32)
    own[...] = small_sum

    def turn(q):
        for k in range(col_blocks):
            tile_t[q, pl.ds(k * block, block), :] = tile[q, :, pl.ds(k * block, block)].T

    repeat(0, cols, turn)

    def add_part(d):
        slot = part_in.at[behind("col", d)]
        send("col", sem_p, d, slot, slot).wait_recv()
        own[...] += part_in[behind("col", d)].astype(F32)

    repeat(1, cols, add_part)
    mixed = own[...]
    pre = split_dot(mixed, w_ref[...], (((1,), (0,)), ((), ())))
    decay = jnp.exp(jnp.minimum(pre, 0.0))
    slope = jnp.where(pre > 0, 1.0, decay)
    up[my_col] = (og_ref[...].astype(F32) * slope).astype(BF16)
    repeat(1, cols, lambda d: send("col", sem_u, d, up.at[my_col], up.at[my_col]).start())
    out_ref[...] = jnp.where(pre > 0, pre, decay - 1.0).astype(BF16)

    scale = 1.0 / math.sqrt(nodes * rows * cols)
    share = width // rows
    over_nodes = (((0,), (0,)), ((), ()))
    upstream = up[my_col]
    term[...] = (split_dot(mixed, upstream, over_nodes) * scale).reshape(rows, share, width)
    repeat(1, rows, lambda d: send("row", sem_w1, d, term.at[ahead("row", d)], w1_in.at[my_row]).start())

    acc[...] = jnp.dot(tile_t[my_col], upstream, preferred_element_type=F32)

    def back(d):
        slot = up.at[behind("col", d)]
        send("col", sem_u, d, slot, slot).wait_recv()
        acc[...] += jnp.dot(
            tile_t[behind("col", d)], up[behind("col", d)], preferred_element_type=F32
        )

    repeat(1, cols // 2, back)

    small[...] = term[my_row]

    def add_w1(d):
        slot = w1_in.at[behind("row", d)]
        send("row", sem_w1, d, slot, slot).wait_recv()
        small[...] += w1_in[behind("row", d)]

    repeat(1, rows, add_w1)
    piece = share // cols
    scattered = piece >= 8 and piece % 8 == 0
    if scattered:

        def send_w2(d):
            src = small.at[pl.ds(pl.multiple_of(ahead("col", d) * piece, piece), piece)]
            send("col", sem_w2, d, src, w2_in.at[my_col]).start()
    else:

        def send_w2(d):
            send("col", sem_w2, d, small, w2_in.at[my_col]).start()

    repeat(1, cols, send_w2)
    repeat(cols // 2, cols, back)

    def scatter_cols(d):
        to = ahead("row", d)
        pc[to] = acc[pl.ds(pl.multiple_of(to * nodes, nodes), nodes), :].astype(BF16)
        send("row", sem_c, d, pc.at[to], pc_in.at[my_row]).start()

    repeat(1, rows, scatter_cols)

    def w2_wait(d):
        slot = w2_in.at[behind("col", d)]
        send("col", sem_w2, d, slot, slot).wait_recv()

    repeat(1, cols, w2_wait)
    if scattered:
        w2_in[my_col] = small[pl.ds(pl.multiple_of(my_col * piece, piece), piece), :]
        w3_in[my_col] = jnp.sum(w2_in[...], axis=0)
        repeat(1, cols, lambda d: send("col", sem_w3, d, w3_in.at[my_col], w3_in.at[my_col]).start())
    else:
        w2_in[my_col] = small[...]
        w4_in[my_row] = jnp.sum(w2_in[...], axis=0)

    grad = acc[pl.ds(pl.multiple_of(my_row * nodes, nodes), nodes), :]
    own[...] = grad

    def add_pc(d):
        slot = pc_in.at[behind("row", d)]
        send("row", sem_c, d, slot, slot).wait_recv()
        own[...] += pc_in[behind("row", d)].astype(F32)

    repeat(1, rows, add_pc)
    ig_ref[...] = split_dot(own[...], w_ref[...], (((1,), (1,)), ((), ()))).astype(BF16)

    if scattered:

        def w3_wait(d):
            slot = w3_in.at[behind("col", d)]
            send("col", sem_w3, d, slot, slot).wait_recv()

        repeat(1, cols, w3_wait)
        w4_in[my_row] = w3_in[...].reshape(share, width)
    repeat(1, rows, lambda d: send("row", sem_w4, d, w4_in.at[my_row], w4_in.at[my_row]).start())

    def w4_wait(d):
        slot = w4_in.at[behind("row", d)]
        send("row", sem_w4, d, slot, slot).wait_recv()

    repeat(1, rows, w4_wait)
    wg_ref[...] = w4_in[...].reshape(width, width)

    def row_sent(d):
        send("row", sem_x, d, x_ref, xg.at[my_row]).wait_send()
        send("row", sem_w1, d, term.at[my_row], w1_in.at[my_row]).wait_send()
        send("row", sem_c, d, pc.at[my_row], pc_in.at[my_row]).wait_send()
        send("row", sem_w4, d, w4_in.at[my_row], w4_in.at[my_row]).wait_send()

    def col_sent(d):
        send("col", sem_p, d, part.at[my_col], part_in.at[my_col]).wait_send()
        send("col", sem_u, d, up.at[my_col], up.at[my_col]).wait_send()
        if scattered:
            send("col", sem_w2, d, small.at[pl.ds(0, piece)], w2_in.at[my_col]).wait_send()
            send("col", sem_w3, d, w3_in.at[my_col], w3_in.at[my_col]).wait_send()
        else:
            send("col", sem_w2, d, small, w2_in.at[my_col]).wait_send()

    repeat(1, rows, row_sent)
    repeat(1, cols, col_sent)


def body(node_features, layer_weight, output_grad, block_values, block_position, tile_count):
    rows, cols = lax.axis_size("row"), lax.axis_size("col")
    nodes, width = node_features.shape
    slots, block = block_values.shape[2], block_values.shape[3]
    assert nodes == block
    share = width // rows
    piece = share // cols
    if not (piece >= 8 and piece % 8 == 0):
        piece = share
    vmem = pl.BlockSpec(memory_space=pltpu.VMEM)
    smem = pl.BlockSpec(memory_space=pltpu.SMEM)
    dma = pltpu.SemaphoreType.DMA
    return pl.pallas_call(
        functools.partial(kernel, rows, cols),
        out_shape=(
            jax.ShapeDtypeStruct((nodes, width), BF16),
            jax.ShapeDtypeStruct((nodes, width), BF16),
            jax.ShapeDtypeStruct((width, width), F32),
        ),
        in_specs=[smem, smem, vmem, vmem, vmem, pl.BlockSpec(memory_space=pl.ANY)],
        out_specs=(vmem, vmem, vmem),
        scratch_shapes=[
            pltpu.VMEM((slots + 1, block, block), BF16),
            pltpu.VMEM((rows, nodes, width), BF16),
            pltpu.VMEM((cols, nodes, rows * nodes), BF16),
            pltpu.VMEM((cols, rows * nodes, nodes), BF16),
            pltpu.VMEM((cols, nodes, width), BF16),
            pltpu.VMEM((cols, nodes, width), BF16),
            pltpu.VMEM((cols, nodes, width), BF16),
            pltpu.VMEM((rows * nodes, width), F32),
            pltpu.VMEM((rows, nodes, width), BF16),
            pltpu.VMEM((rows, nodes, width), BF16),
            pltpu.VMEM((rows, share, width), F32),
            pltpu.VMEM((rows, share, width), F32),
            pltpu.VMEM((nodes, width), F32),
            pltpu.VMEM((cols, piece, width), F32),
            pltpu.VMEM((share, width), F32),
            pltpu.VMEM((cols, piece, width), F32),
            pltpu.VMEM((rows, share, width), F32),
            dma,
            dma((2, rows - 1)),
            dma((2, cols - 1)),
            dma((2, cols - 1)),
            dma((2, rows - 1)),
            dma((2, rows - 1)),
            dma((2, cols - 1)),
            dma((2, cols - 1)),
            dma((2, rows - 1)),
        ],
        compiler_params=pltpu.CompilerParams(collective_id=0, has_side_effects=True),
    )(
        block_position.reshape(slots),
        tile_count.reshape(1),
        node_features,
        layer_weight,
        output_grad,
        block_values.reshape(slots, block, block),
    )


def solution(mesh):
    in_specs = (
        P(("row", "col"), None),
        P(),
        P(("row", "col"), None),
        P("row", "col", None, None, None),
        P("row", "col", None),
        P("row", "col"),
    )
    out_specs = (P(("row", "col"), None), P(("row", "col"), None), P())
    return jax.shard_map(body, mesh=mesh, in_specs=in_specs, out_specs=out_specs, check_vma=False)
```

time: 278 us -> 56.3 us (0.20)
  waiting for transfers between devices: 198 us -> 0 us
  Pallas kernels: 0 us -> 51.1 us
  blocking collectives: 45.6 us -> 0 us
  between operations: 14.6 us -> 1.3 us
  other arithmetic: 8.59 us -> 0 us
  matrix products: 5.27 us -> 0 us
    psum x2 -> x0, waiting for transfers between devices: 172 us -> none  [the longest x1 129 us: body(): weight_grad = lax.psum(weight_term, ('row', 'col'))]
    pallas_call x0 -> x1, Pallas kernels: none -> 51.1 us  [body(): pl.pallas_call(functools.partial(kernel, rows, cols), out_shape=(jax.Shap...]
    all_gather x2 -> x0, blocking collectives: 45.6 us -> none  [the longest x1 38.4 us: body(): grad_panel = lax.all_gather(output_grad, 'col', axis=0, tiled=True)]
    reduce_scatter x1 -> x0, waiting for transfers between devices: 25.7 us -> none  [body(): lax.psum_scatter(partial_cols.astype(jnp.bfloat16), 'row', scatter_dimens...]
    dot_general x5 -> x0, matrix products: 5.27 us -> none  [the longest x1 1.75 us: body(): jnp.einsum('nf,ng->fg', node_features.astype(jnp.float32), column_grad, p...]
    convert_element_type x5 -> x0, other arithmetic: 3.69 us -> none  [the longest x1 1.34 us: body(): (grad_panel.astype(jnp.float32) * elu_slope(summed)).astype(jnp.bfloat16)]
  transfers between devices with their start and end apart: 3 -> 0, of which waited for: 3 -> 0; matrix products, arithmetic and copies ran while one was open for 1% -> 0% of each run, Pallas kernels for 0% -> 0%
where the time goes in v1:
time: 56.3 us; the launch traced here: 56.1 us
  Pallas kernels  51.1 us (91%)
  local copies, waits for them, and re-layouts  3.69 us (7%)
  between operations  1.3 us (2%)
    pallas_call x1, Pallas kernels, body(): pl.pallas_call(functools.partial(kernel, rows, cols), out_shape=(jax.Shap...  51.1 us
    unnamed x5, local copies, waits for them, and re-layouts  3.69 us

profile of v1, /device:TPU:0, one launch (start us, length us, event | category | flops | bytes accessed | tf_op | source)
XLA Modules:
  0.0 56.1 jit_solution(1885836930822272459)
XLA Ops:
  1.3 51.1 %shard_map.85 = (bf16[128,256]{1,0:T(8,128)(2,1)}, bf16[128,256]{1,0:T(8,128)(2,1)}, f32[256,256]{1,0:T(8,128)}) custom-call(s32[24]{0:T(128)} %bitcast.5, s32[1]{0:T(128)} %bitcast.3.count, bf16[128,256]{1,0:T(8,128)(2,1)} %x_ref.1, bf16[256,256]{1,0:T(8,128)(2,1)} %w_ref.1, bf16[128,256]{1,0:T(8,128)(2,1)} %og_ref.1, bf16[24,128,128]{2,1,0:T(8,128)(2,1)} %bitcast.4), custom_call_target="tpu_custom_call" | custom-call | tf_op jit(solution)/shard_map/pallas_call | solution.py:293
  52.4 0.0 copy-start
  52.4 1.5 %copy.13 = bf16[128,256]{1,0:T(8,128)(2,1)} copy(bf16[128,256]{1,0:T(8,128)(2,1)} %get-tuple-element.6) | data formatting | bytes 131072
  53.9 1.5 %copy.14 = bf16[128,256]{1,0:T(8,128)(2,1)} copy(bf16[128,256]{1,0:T(8,128)(2,1)} %get-tuple-element.7) | data formatting | bytes 131072
  55.4 0.0 copy-done
  55.4 0.7 %copy.15 = f32[256,256]{1,0:T(8,128)} copy(f32[256,256]{1,0:T(8,128)S(1)} %copy-done) | data formatting | bytes 524288
Async XLA Ops:
  52.4 3.0 %copy-start = (f32[256,256]{1,0:T(8,128)S(1)}, f32[256,256]{1,0:T(8,128)}, u32[]{:S(2)}) copy-start(f32[256,256]{1,0:T(8,128)} %get-tuple-element.8) | copy-start | bytes 786436

commit v2 on v1

v2 whole, which is shorter than its diff:
```python
import functools
import math

import jax
import jax.numpy as jnp
from jax import lax
from jax.experimental import pallas as pl
from jax.experimental.pallas import tpu as pltpu
from jax.sharding import PartitionSpec as P

MESH = pl.DeviceIdType.MESH
F32 = jnp.float32
BF16 = jnp.bfloat16


def repeat(steps, step):
    if len(steps) <= 8:
        for d in steps:
            step(d)
    else:

        def one(d, unused):
            step(d)
            return unused

        lax.fori_loop(min(steps), max(steps) + 1, one, 0)


def split_dot(left, right, dims):
    high = left.astype(BF16)
    low = (left - high.astype(F32)).astype(BF16)
    first = lax.dot_general(high, right, dims, preferred_element_type=F32)
    return first + lax.dot_general(low, right, dims, preferred_element_type=F32)


def kernel(
    rows,
    cols,
    position,
    count,
    x_hbm,
    w_hbm,
    og_hbm,
    values_hbm,
    out_hbm,
    ig_hbm,
    wg_hbm,
    values,
    w_ref,
    og_ref,
    out_ref,
    ig_ref,
    wg_ref,
    xg,
    tile,
    tile_t,
    mate_part,
    mate_in,
    part,
    part_in,
    up,
    acc,
    pc,
    pc_in,
    term,
    w1_in,
    own,
    w2_in,
    small,
    w3_in,
    w4_in,
    sem_v,
    sem_x,
    sem_y,
    sem_z,
    sem_u,
    sem_f,
    sem_c,
    sem_w1,
    sem_w2,
    sem_w3,
    sem_w4,
):
    nodes, width = x_hbm.shape
    slots, block = values_hbm.shape[0], values_hbm.shape[1]
    col_blocks = rows
    my_row = lax.axis_index("row")
    my_col = lax.axis_index("col")
    size = {"row": rows, "col": cols}
    me = {"row": my_row, "col": my_col}
    half = cols // 2
    my_high = my_col // 2
    my_low = lax.rem(my_col, 2)
    mate = my_high * 2 + 1 - my_low
    others = [half // 2] + [d for d in range(1, half) if d != half // 2]
    row_steps = list(range(1, rows))
    col_steps = list(range(1, cols))

    def ahead(axis, d):
        return lax.rem(me[axis] + d, size[axis])

    def behind(axis, d):
        return lax.rem(me[axis] + size[axis] - d, size[axis])

    def high_ahead(d):
        return lax.rem(my_high + d, half)

    def high_behind(d):
        return lax.rem(my_high + half - d, half)

    def move(sem, index, src, dst, **target):
        return pltpu.make_async_remote_copy(
            src_ref=src,
            dst_ref=dst,
            send_sem=sem.at[0, index],
            recv_sem=sem.at[1, index],
            device_id=target,
            device_id_type=MESH,
        )

    def send(axis, sem, d, src, dst):
        return move(sem, d - 1, src, dst, **{axis: ahead(axis, d)})

    load = pltpu.make_async_copy(values_hbm, values.at[pl.ds(0, slots)], sem_v.at[0])
    load_x = pltpu.make_async_copy(x_hbm, xg.at[my_row], sem_v.at[1])
    load_w = pltpu.make_async_copy(w_hbm, w_ref, sem_v.at[2])
    load_og = pltpu.make_async_copy(og_hbm, og_ref, sem_v.at[3])
    for one in (load, load_x, load_w, load_og):
        one.start()

    barrier = pltpu.get_barrier_semaphore()
    for axis in ("col", "row"):

        def greet(d, axis=axis):
            pl.semaphore_signal(
                barrier, inc=1, device_id={axis: ahead(axis, d)}, device_id_type=MESH
            )

        repeat(list(range(1, size[axis])), greet)
    values[slots] = jnp.zeros((block, block), BF16)
    pl.semaphore_wait(barrier, rows + cols - 2)

    repeat(row_steps, lambda d: send("row", sem_x, d, x_hbm, xg.at[my_row]).start())

    load.wait()
    live_count = count[0, 0]

    def build(q, pointer):
        for k in range(col_blocks):
            here = position[jnp.minimum(pointer, slots - 1)]
            live = (here == q * col_blocks + k) & (pointer < live_count)
            slot = jnp.where(live, pointer, slots)
            tile[q, :, pl.ds(k * block, block)] = values[slot]
            pointer = pointer + live.astype(jnp.int32)
        return pointer

    if cols <= 8:
        pointer = jnp.int32(0)
        for q in range(cols):
            pointer = build(q, pointer)
    else:
        lax.fori_loop(0, cols, build, jnp.int32(0))

    load_x.wait()

    def from_row(d):
        slot = xg.at[behind("row", d)]
        send("row", sem_x, d, slot, slot).wait_recv()

    repeat(row_steps, from_row)
    panel = xg[...].reshape(rows * nodes, width)

    def to_mate(d):
        high = high_ahead(d)
        product = jnp.dot(tile[high * 2 + 1 - my_low], panel, preferred_element_type=F32)
        mate_part[high] = product.astype(BF16)
        move(sem_y, d, mate_part.at[high], mate_in.at[high], col=mate).start()

    repeat(others, to_mate)
    to_mate(0)

    def from_mate(d):
        high = high_ahead(d)
        product = jnp.dot(tile[high * 2 + my_low], panel, preferred_element_type=F32)
        slot = mate_in.at[high]
        move(sem_y, d, slot, slot, col=mate).wait_recv()
        return product + mate_in[high].astype(F32)

    def to_high(d):
        high = high_ahead(d)
        part[high] = from_mate(d).astype(BF16)
        move(sem_z, d - 1, part.at[high], part_in.at[my_high], col=high * 2 + my_low).start()

    repeat(others, to_high)
    own[...] = from_mate(0)

    def turn(q):
        for k in range(col_blocks):
            tile_t[q, pl.ds(k * block, block), :] = tile[q, :, pl.ds(k * block, block)].T

    repeat(list(range(cols)), turn)

    def add_part(d):
        high = high_behind(d)
        slot = part_in.at[high]
        move(sem_z, d - 1, slot, slot, col=high * 2 + my_low).wait_recv()
        own[...] += part_in[high].astype(F32)

    load_w.wait()
    load_og.wait()
    repeat(others, add_part)
    mixed = own[...]
    pre = split_dot(mixed, w_ref[...], (((1,), (0,)), ((), ())))
    decay = jnp.exp(jnp.minimum(pre, 0.0))
    slope = jnp.where(pre > 0, 1.0, decay)
    up[my_col] = (og_ref[...].astype(F32) * slope).astype(BF16)

    def up_high(d):
        move(sem_u, d - 1, up.at[my_col], up.at[my_col], col=high_ahead(d) * 2 + my_low).start()

    move(sem_f, 0, up.at[my_col], up.at[my_col], col=mate).start()
    repeat(others, up_high)
    out_ref[...] = jnp.where(pre > 0, pre, decay - 1.0).astype(BF16)
    save_out = pltpu.make_async_copy(out_ref, out_hbm, sem_v.at[4])
    save_out.start()

    scale = 1.0 / math.sqrt(nodes * rows * cols)
    share = width // rows
    over_nodes = (((0,), (0,)), ((), ()))
    upstream = up[my_col]
    term[...] = (split_dot(mixed, upstream, over_nodes) * scale).reshape(rows, share, width)
    repeat(
        row_steps,
        lambda d: send("row", sem_w1, d, term.at[ahead("row", d)], w1_in.at[my_row]).start(),
    )

    acc[...] = jnp.dot(tile_t[my_col], upstream, preferred_element_type=F32)

    def back(source):
        acc[...] += jnp.dot(tile_t[source], up[source], preferred_element_type=F32)

    def back_high(d):
        source = high_behind(d) * 2 + my_low
        slot = up.at[source]
        move(sem_u, d - 1, slot, slot, col=source).wait_recv()
        move(sem_f, d, slot, slot, col=mate).start()
        back(source)

    def back_mate(d):
        source = high_behind(d) * 2 + 1 - my_low
        slot = up.at[source]
        move(sem_f, d, slot, slot, col=mate).wait_recv()
        back(source)

    back_mate(0)

    small[...] = term[my_row]

    def add_w1(d):
        slot = w1_in.at[behind("row", d)]
        send("row", sem_w1, d, slot, slot).wait_recv()
        small[...] += w1_in[behind("row", d)]

    repeat(row_steps, add_w1)
    piece = share // cols
    scattered = piece >= 8 and piece % 8 == 0
    if scattered:

        def send_w2(d):
            src = small.at[pl.ds(pl.multiple_of(ahead("col", d) * piece, piece), piece)]
            send("col", sem_w2, d, src, w2_in.at[my_col]).start()
    else:

        def send_w2(d):
            send("col", sem_w2, d, small, w2_in.at[my_col]).start()

    repeat(col_steps, send_w2)

    def w2_wait(d):
        slot = w2_in.at[behind("col", d)]
        send("col", sem_w2, d, slot, slot).wait_recv()

    repeat(others, back_high)
    repeat(col_steps, w2_wait)
    if scattered:
        w2_in[my_col] = small[pl.ds(pl.multiple_of(my_col * piece, piece), piece), :]
        w3_in[my_col] = jnp.sum(w2_in[...], axis=0)
        repeat(
            col_steps,
            lambda d: send("col", sem_w3, d, w3_in.at[my_col], w3_in.at[my_col]).start(),
        )
    else:
        w2_in[my_col] = small[...]
        w4_in[my_row] = jnp.sum(w2_in[...], axis=0)

    repeat(others, back_mate)

    def scatter_cols(d):
        to = ahead("row", d)
        pc[to] = acc[pl.ds(pl.multiple_of(to * nodes, nodes), nodes), :].astype(BF16)
        send("row", sem_c, d, pc.at[to], pc_in.at[my_row]).start()

    repeat(row_steps, scatter_cols)

    if scattered:

        def w3_wait(d):
            slot = w3_in.at[behind("col", d)]
            send("col", sem_w3, d, slot, slot).wait_recv()

        repeat(col_steps, w3_wait)
        w4_in[my_row] = w3_in[...].reshape(share, width)
    repeat(
        row_steps, lambda d: send("row", sem_w4, d, w4_in.at[my_row], w4_in.at[my_row]).start()
    )

    own[...] = acc[pl.ds(pl.multiple_of(my_row * nodes, nodes), nodes), :]

    def add_pc(d):
        slot = pc_in.at[behind("row", d)]
        send("row", sem_c, d, slot, slot).wait_recv()
        own[...] += pc_in[behind("row", d)].astype(F32)

    repeat(row_steps, add_pc)
    ig_ref[...] = split_dot(own[...], w_ref[...], (((1,), (1,)), ((), ()))).astype(BF16)
    save_ig = pltpu.make_async_copy(ig_ref, ig_hbm, sem_v.at[5])
    save_ig.start()

    def row_sent(d):
        send("row", sem_x, d, x_hbm, xg.at[my_row]).wait_send()
        send("row", sem_w1, d, term.at[my_row], w1_in.at[my_row]).wait_send()
        send("row", sem_c, d, pc.at[my_row], pc_in.at[my_row]).wait_send()
        send("row", sem_w4, d, w4_in.at[my_row], w4_in.at[my_row]).wait_send()

    def col_sent(d):
        if scattered:
            send("col", sem_w2, d, small.at[pl.ds(0, piece)], w2_in.at[my_col]).wait_send()
            send("col", sem_w3, d, w3_in.at[my_col], w3_in.at[my_col]).wait_send()
        else:
            send("col", sem_w2, d, small, w2_in.at[my_col]).wait_send()

    def mate_sent(d):
        move(sem_y, d, mate_part.at[0], mate_in.at[0], col=mate).wait_send()
        move(sem_f, d, up.at[my_col], up.at[my_col], col=mate).wait_send()

    def high_sent(d):
        move(sem_z, d - 1, part.at[0], part_in.at[0], col=mate).wait_send()
        move(sem_u, d - 1, up.at[my_col], up.at[my_col], col=mate).wait_send()

    repeat(list(range(half)), mate_sent)
    repeat(list(range(1, half)), high_sent)
    repeat(col_steps, col_sent)

    def w4_wait(d):
        slot = w4_in.at[behind("row", d)]
        send("row", sem_w4, d, slot, slot).wait_recv()

    repeat(row_steps, w4_wait)
    wg_ref[...] = w4_in[...].reshape(width, width)
    save_wg = pltpu.make_async_copy(wg_ref, wg_hbm, sem_v.at[6])
    save_wg.start()
    repeat(row_steps, row_sent)
    save_out.wait()
    save_ig.wait()
    save_wg.wait()


def body(node_features, layer_weight, output_grad, block_values, block_position, tile_count):
    rows, cols = lax.axis_size("row"), lax.axis_size("col")
    nodes, width = node_features.shape
    slots, block = block_values.shape[2], block_values.shape[3]
    assert nodes == block
    share = width // rows
    piece = share // cols
    if not (piece >= 8 and piece % 8 == 0):
        piece = share
    place = pl.BlockSpec(memory_space=pl.ANY)
    half = cols // 2
    assert cols == 2 * half
    smem = pl.BlockSpec(memory_space=pltpu.SMEM)
    dma = pltpu.SemaphoreType.DMA
    return pl.pallas_call(
        functools.partial(kernel, rows, cols),
        out_shape=(
            jax.ShapeDtypeStruct((nodes, width), BF16),
            jax.ShapeDtypeStruct((nodes, width), BF16),
            jax.ShapeDtypeStruct((width, width), F32),
        ),
        in_specs=[smem, smem, place, place, place, place],
        out_specs=(place, place, place),
        scratch_shapes=[
            pltpu.VMEM((slots + 1, block, block), BF16),
            pltpu.VMEM((width, width), BF16),
            pltpu.VMEM((nodes, width), BF16),
            pltpu.VMEM((nodes, width), BF16),
            pltpu.VMEM((nodes, width), BF16),
            pltpu.VMEM((width, width), F32),
            pltpu.VMEM((rows, nodes, width), BF16),
            pltpu.VMEM((cols, nodes, rows * nodes), BF16),
            pltpu.VMEM((cols, rows * nodes, nodes), BF16),
            pltpu.VMEM((half, nodes, width), BF16),
            pltpu.VMEM((half, nodes, width), BF16),
            pltpu.VMEM((half, nodes, width), BF16),
            pltpu.VMEM((half, nodes, width), BF16),
            pltpu.VMEM((cols, nodes, width), BF16),
            pltpu.VMEM((rows * nodes, width), F32),
            pltpu.VMEM((rows, nodes, width), BF16),
            pltpu.VMEM((rows, nodes, width), BF16),
            pltpu.VMEM((rows, share, width), F32),
            pltpu.VMEM((rows, share, width), F32),
            pltpu.VMEM((nodes, width), F32),
            pltpu.VMEM((cols, piece, width), F32),
            pltpu.VMEM((share, width), F32),
            pltpu.VMEM((cols, piece, width), F32),
            pltpu.VMEM((rows, share, width), F32),
            dma((7,)),
            dma((2, rows - 1)),
            dma((2, half)),
            dma((2, half - 1)),
            dma((2, half - 1)),
            dma((2, half)),
            dma((2, rows - 1)),
            dma((2, rows - 1)),
            dma((2, cols - 1)),
            dma((2, cols - 1)),
            dma((2, rows - 1)),
        ],
        compiler_params=pltpu.CompilerParams(collective_id=0, has_side_effects=True),
    )(
        block_position.reshape(slots),
        tile_count,
        node_features,
        layer_weight,
        output_grad,
        block_values.reshape(slots, block, block),
    )


def solution(mesh):
    in_specs = (
        P(("row", "col"), None),
        P(),
        P(("row", "col"), None),
        P("row", "col", None, None, None),
        P("row", "col", None),
        P("row", "col"),
    )
    out_specs = (P(("row", "col"), None), P(("row", "col"), None), P())
    return jax.shard_map(body, mesh=mesh, in_specs=in_specs, out_specs=out_specs, check_vma=False)
```

time: 56.3 us -> 48.4 us (0.86)
  Pallas kernels: 51.1 us -> 42.9 us
    pallas_call x1, Pallas kernels: 51.1 us -> 42.9 us  [body(): pl.pallas_call(functools.partial(kernel, rows, cols), out_shape=(jax.Shap...]
where the time goes in v2:
time: 48.4 us; the launch traced here: 47.9 us
  Pallas kernels  42.9 us (89%)
  local copies, waits for them, and re-layouts  3.69 us (8%)
  between operations  1.3 us (3%)
    pallas_call x1, Pallas kernels, body(): pl.pallas_call(functools.partial(kernel, rows, cols), out_shape=(jax.Shap...  42.9 us
    unnamed x5, local copies, waits for them, and re-layouts  3.69 us

profile of v2, /device:TPU:0, one launch (start us, length us, event | category | flops | bytes accessed | tf_op | source)
XLA Modules:
  0.0 47.9 jit_solution(12123265760026947598)
XLA Ops:
  1.3 42.9 %shard_map.85 = (bf16[128,256]{1,0:T(8,128)(2,1)}, bf16[128,256]{1,0:T(8,128)(2,1)}, f32[256,256]{1,0:T(8,128)}) custom-call(s32[24]{0:T(128)} %bitcast.3, s32[1,1]{1,0:T(1,128)S(6)} %copy.12.count, bf16[128,256]{1,0:T(8,128)(2,1)} %x_hbm.1, bf16[256,256]{1,0:T(8,128)(2,1)} %w_hbm.1, bf16[128,256]{1,0:T(8,128)(2,1)} %og_hbm.1, bf16[24,128,128]{2,1,0:T(8,128)(2,1)} %bitcast.2), custom_call_target="tpu_custom_call" | custom-call | tf_op jit(solution)/shard_map/pallas_call | solution.py:382
  44.2 0.0 copy-start
  44.2 1.5 %copy.13 = bf16[128,256]{1,0:T(8,128)(2,1)} copy(bf16[128,256]{1,0:T(8,128)(2,1)} %get-tuple-element.6) | data formatting | bytes 131072
  45.7 1.5 %copy.14 = bf16[128,256]{1,0:T(8,128)(2,1)} copy(bf16[128,256]{1,0:T(8,128)(2,1)} %get-tuple-element.7) | data formatting | bytes 131072
  47.2 0.0 copy-done
  47.2 0.7 %copy.15 = f32[256,256]{1,0:T(8,128)} copy(f32[256,256]{1,0:T(8,128)S(1)} %copy-done) | data formatting | bytes 524288
Async XLA Ops:
  44.2 3.0 %copy-start = (f32[256,256]{1,0:T(8,128)S(1)}, f32[256,256]{1,0:T(8,128)}, u32[]{:S(2)}) copy-start(f32[256,256]{1,0:T(8,128)} %get-tuple-element.8) | copy-start | bytes 786436

commit v3 on v2

--- a/solution.py
+++ b/solution.py
@@ -42,15 +42,12 @@
     w_hbm,
     og_hbm,
     values_hbm,
-    out_hbm,
-    ig_hbm,
-    wg_hbm,
+    out_ref,
+    ig_ref,
+    wg_ref,
     values,
     w_ref,
     og_ref,
-    out_ref,
-    ig_ref,
-    wg_ref,
     xg,
     tile,
     tile_t,
@@ -221,14 +218,12 @@
     move(sem_f, 0, up.at[my_col], up.at[my_col], col=mate).start()
     repeat(others, up_high)
     out_ref[...] = jnp.where(pre > 0, pre, decay - 1.0).astype(BF16)
-    save_out = pltpu.make_async_copy(out_ref, out_hbm, sem_v.at[4])
-    save_out.start()
 
     scale = 1.0 / math.sqrt(nodes * rows * cols)
     share = width // rows
     over_nodes = (((0,), (0,)), ((), ()))
     upstream = up[my_col]
-    term[...] = (split_dot(mixed, upstream, over_nodes) * scale).reshape(rows, share, width)
+    term[...] = (split_dot(mixed, upstream, over_nodes) * scale).reshape(rows, share, width).astype(BF16)
     repeat(
         row_steps,
         lambda d: send("row", sem_w1, d, term.at[ahead("row", d)], w1_in.at[my_row]).start(),
@@ -254,12 +249,12 @@
 
     back_mate(0)
 
-    small[...] = term[my_row]
+    small[...] = term[my_row].astype(F32)
 
     def add_w1(d):
         slot = w1_in.at[behind("row", d)]
         send("row", sem_w1, d, slot, slot).wait_recv()
-        small[...] += w1_in[behind("row", d)]
+        small[...] += w1_in[behind("row", d)].astype(F32)
 
     repeat(row_steps, add_w1)
     piece = share // cols
@@ -291,7 +286,7 @@
         )
     else:
         w2_in[my_col] = small[...]
-        w4_in[my_row] = jnp.sum(w2_in[...], axis=0)
+        w4_in[my_row] = jnp.sum(w2_in[...], axis=0).astype(BF16)
 
     repeat(others, back_mate)
 
@@ -309,7 +304,7 @@
             send("col", sem_w3, d, slot, slot).wait_recv()
 
         repeat(col_steps, w3_wait)
-        w4_in[my_row] = w3_in[...].reshape(share, width)
+        w4_in[my_row] = w3_in[...].reshape(share, width).astype(BF16)
     repeat(
         row_steps, lambda d: send("row", sem_w4, d, w4_in.at[my_row], w4_in.at[my_row]).start()
     )
@@ -323,8 +318,6 @@
 
     repeat(row_steps, add_pc)
     ig_ref[...] = split_dot(own[...], w_ref[...], (((1,), (1,)), ((), ()))).astype(BF16)
-    save_ig = pltpu.make_async_copy(ig_ref, ig_hbm, sem_v.at[5])
-    save_ig.start()
 
     def row_sent(d):
         send("row", sem_x, d, x_hbm, xg.at[my_row]).wait_send()
@@ -356,13 +349,17 @@
         send("row", sem_w4, d, slot, slot).wait_recv()
 
     repeat(row_steps, w4_wait)
-    wg_ref[...] = w4_in[...].reshape(width, width)
-    save_wg = pltpu.make_async_copy(wg_ref, wg_hbm, sem_v.at[6])
-    save_wg.start()
+    wg_ref[...] = w4_in[...].reshape(width, width).astype(F32)
     repeat(row_steps, row_sent)
-    save_out.wait()
-    save_ig.wait()
-    save_wg.wait()
+
+
+def finish(out_ref, ig_ref, wg_ref, out_hbm, ig_hbm, wg_hbm, sem):
+    trio = ((out_ref, out_hbm), (ig_ref, ig_hbm), (wg_ref, wg_hbm))
+    copies = [pltpu.make_async_copy(a, b, sem.at[i]) for i, (a, b) in enumerate(trio)]
+    for copy in copies:
+        copy.start()
+    for copy in copies:
+        copy.wait()
 
 
 def body(node_features, layer_weight, output_grad, block_values, block_position, tile_count):
@@ -375,26 +372,29 @@
     if not (piece >= 8 and piece % 8 == 0):
         piece = share
     place = pl.BlockSpec(memory_space=pl.ANY)
+    inside = pl.BlockSpec(memory_space=pltpu.VMEM)
     half = cols // 2
     assert cols == 2 * half
     smem = pl.BlockSpec(memory_space=pltpu.SMEM)
     dma = pltpu.SemaphoreType.DMA
-    return pl.pallas_call(
+    shapes = (
+        jax.ShapeDtypeStruct((nodes, width), BF16),
+        jax.ShapeDtypeStruct((nodes, width), BF16),
+        jax.ShapeDtypeStruct((width, width), F32),
+    )
+    results = pl.pallas_call(
         functools.partial(kernel, rows, cols),
         out_shape=(
-            jax.ShapeDtypeStruct((nodes, width), BF16),
-            jax.ShapeDtypeStruct((nodes, width), BF16),
-            jax.ShapeDtypeStruct((width, width), F32),
+            pltpu.VMEM((nodes, width), BF16),
+            pltpu.VMEM((nodes, width), BF16),
+            pltpu.VMEM((width, width), F32),
         ),
         in_specs=[smem, smem, place, place, place, place],
-        out_specs=(place, place, place),
+        out_specs=(inside, inside, inside),
         scratch_shapes=[
             pltpu.VMEM((slots + 1, block, block), BF16),
             pltpu.VMEM((width, width), BF16),
             pltpu.VMEM((nodes, width), BF16),
-            pltpu.VMEM((nodes, width), BF16),
-            pltpu.VMEM((nodes, width), BF16),
-            pltpu.VMEM((width, width), F32),
             pltpu.VMEM((rows, nodes, width), BF16),
             pltpu.VMEM((cols, nodes, rows * nodes), BF16),
             pltpu.VMEM((cols, rows * nodes, nodes), BF16),
@@ -406,13 +406,13 @@
             pltpu.VMEM((rows * nodes, width), F32),
             pltpu.VMEM((rows, nodes, width), BF16),
             pltpu.VMEM((rows, nodes, width), BF16),
-            pltpu.VMEM((rows, share, width), F32),
-            pltpu.VMEM((rows, share, width), F32),
+            pltpu.VMEM((rows, share, width), BF16),
+            pltpu.VMEM((rows, share, width), BF16),
             pltpu.VMEM((nodes, width), F32),
             pltpu.VMEM((cols, piece, width), F32),
             pltpu.VMEM((share, width), F32),
             pltpu.VMEM((cols, piece, width), F32),
-            pltpu.VMEM((rows, share, width), F32),
+            pltpu.VMEM((rows, share, width), BF16),
             dma((7,)),
             dma((2, rows - 1)),
             dma((2, half)),
@@ -434,6 +434,16 @@
         output_grad,
         block_values.reshape(slots, block, block),
     )
+    return pl.pallas_call(
+        finish,
+        out_shape=shapes,
+        in_specs=[inside] * 3,
+        out_specs=(place,) * 3,
+        scratch_shapes=[
+            dma((3,)),
+        ],
+        compiler_params=pltpu.CompilerParams(vmem_limit_bytes=4 << 20),
+    )(*results)
 
 
 def solution(mesh):

time: 48.4 us -> 41.4 us (0.86)
  local copies, waits for them, and re-layouts: 3.69 us -> 0 us
  Pallas kernels: 42.9 us -> 39.9 us
    unnamed x5 -> x0, local copies, waits for them, and re-layouts: 3.69 us -> none
    pallas_call x1 -> x2, Pallas kernels: 42.9 us -> 39.9 us  [the longest x1 39.1 us: body(): pl.pallas_call(functools.partial(kernel, rows, cols), out_shape=(pltpu.VM...]
where the time goes in v3:
time: 41.4 us; the launch traced here: 41.2 us
  Pallas kernels  39.9 us (96%)
  between operations  1.29 us (3%)
    pallas_call x1, Pallas kernels, body(): pl.pallas_call(functools.partial(kernel, rows, cols), out_shape=(pltpu.VM...  39.1 us

profile of v3, /device:TPU:0, one launch (start us, length us, event | category | flops | bytes accessed | tf_op | source)
XLA Modules:
  0.0 41.2 jit_solution(4625738316767530483)
XLA Ops:
  1.3 39.1 %shard_map.85 = (bf16[128,256]{1,0:T(8,128)(2,1)S(1)}, bf16[128,256]{1,0:T(8,128)(2,1)S(1)}, f32[256,256]{1,0:T(8,128)S(1)}) custom-call(s32[24]{0:T(128)} %bitcast.3, s32[1,1]{1,0:T(1,128)S(6)} %copy.9.count, bf16[128,256]{1,0:T(8,128)(2,1)} %x_hbm.1, bf16[256,256]{1,0:T(8,128)(2,1)} %w_hbm.1, bf16[128,256]{1,0:T(8,128)(2,1)} %og_hbm.1, ...), custom_call_target="tpu_custom_call" | custom-call | tf_op jit(solution)/shard_map/pallas_call | solution.py:385
  40.4 0.8 %shard_map.86 = (bf16[128,256]{1,0:T(8,128)(2,1)}, bf16[128,256]{1,0:T(8,128)(2,1)}, f32[256,256]{1,0:T(8,128)}) custom-call(bf16[128,256]{1,0:T(8,128)(2,1)S(1)} %get-tuple-element.6.out_ref, bf16[128,256]{1,0:T(8,128)(2,1)S(1)} %get-tuple-element.7.ig_ref, f32[256,256]{1,0:T(8,128)S(1)} %get-tuple-element.8.wg_ref), custom_call_target="tpu_custom_call" | custom-call | tf_op jit(solution)/shard_map/pallas_call | solution.py:437

commit v4 on v3

--- a/solution.py
+++ b/solution.py
@@ -36,8 +36,8 @@
 def kernel(
     rows,
     cols,
-    position,
-    count,
+    position_hbm,
+    count_hbm,
     x_hbm,
     w_hbm,
     og_hbm,
@@ -45,6 +45,8 @@
     out_ref,
     ig_ref,
     wg_ref,
+    position,
+    count,
     values,
     w_ref,
     og_ref,
@@ -90,6 +92,8 @@
     my_low = lax.rem(my_col, 2)
     mate = my_high * 2 + 1 - my_low
     others = [half // 2] + [d for d in range(1, half) if d != half // 2]
+    pieces = [pl.ds(p * nodes // 2, nodes // 2) for p in range(2)]
+    count_pieces = len(pieces)
     row_steps = list(range(1, rows))
     col_steps = list(range(1, cols))
 
@@ -122,23 +126,26 @@
     load_x = pltpu.make_async_copy(x_hbm, xg.at[my_row], sem_v.at[1])
     load_w = pltpu.make_async_copy(w_hbm, w_ref, sem_v.at[2])
     load_og = pltpu.make_async_copy(og_hbm, og_ref, sem_v.at[3])
-    for one in (load, load_x, load_w, load_og):
+    load_position = pltpu.make_async_copy(position_hbm, position, sem_v.at[4])
+    load_count = pltpu.make_async_copy(count_hbm, count, sem_v.at[5])
+    for one in (load_position, load_count, load, load_x, load_w, load_og):
         one.start()
 
     barrier = pltpu.get_barrier_semaphore()
-    for axis in ("col", "row"):
-
-        def greet(d, axis=axis):
-            pl.semaphore_signal(
-                barrier, inc=1, device_id={axis: ahead(axis, d)}, device_id_type=MESH
-            )
-
-        repeat(list(range(1, size[axis])), greet)
+
+    def greet(**target):
+        pl.semaphore_signal(barrier, inc=1, device_id=target, device_id_type=MESH)
+
+    repeat(others, lambda d: greet(col=high_ahead(d) * 2 + my_low))
+    greet(col=mate)
+    repeat(row_steps, lambda d: greet(row=ahead("row", d)))
     values[slots] = jnp.zeros((block, block), BF16)
-    pl.semaphore_wait(barrier, rows + cols - 2)
+    pl.semaphore_wait(barrier, rows + half - 1)
 
     repeat(row_steps, lambda d: send("row", sem_x, d, x_hbm, xg.at[my_row]).start())
 
+    load_position.wait()
+    load_count.wait()
     load.wait()
     live_count = count[0, 0]
 
@@ -171,25 +178,41 @@
         high = high_ahead(d)
         product = jnp.dot(tile[high * 2 + 1 - my_low], panel, preferred_element_type=F32)
         mate_part[high] = product.astype(BF16)
-        move(sem_y, d, mate_part.at[high], mate_in.at[high], col=mate).start()
+        for p, some in enumerate(pieces):
+            index = d * count_pieces + p
+            move(sem_y, index, mate_part.at[high, some], mate_in.at[high, some], col=mate).start()
 
     repeat(others, to_mate)
     to_mate(0)
 
-    def from_mate(d):
+    def from_mate(d, take):
         high = high_ahead(d)
-        product = jnp.dot(tile[high * 2 + my_low], panel, preferred_element_type=F32)
-        slot = mate_in.at[high]
-        move(sem_y, d, slot, slot, col=mate).wait_recv()
-        return product + mate_in[high].astype(F32)
+        own[...] = jnp.dot(tile[high * 2 + my_low], panel, preferred_element_type=F32)
+        for p, some in enumerate(pieces):
+            slot = mate_in.at[high, some]
+            move(sem_y, d * count_pieces + p, slot, slot, col=mate).wait_recv()
+            take(p, some, own[some] + mate_in[high, some].astype(F32))
 
     def to_high(d):
         high = high_ahead(d)
-        part[high] = from_mate(d).astype(BF16)
-        move(sem_z, d - 1, part.at[high], part_in.at[my_high], col=high * 2 + my_low).start()
+
+        def take(p, some, total):
+            part[high, some] = total.astype(BF16)
+            move(
+                sem_z,
+                (d - 1) * count_pieces + p,
+                part.at[high, some],
+                part_in.at[my_high, some],
+                col=high * 2 + my_low,
+            ).start()
+
+        from_mate(d, take)
+
+    def keep(p, some, total):
+        own[some] = total
 
     repeat(others, to_high)
-    own[...] = from_mate(0)
+    from_mate(0, keep)
 
     def turn(q):
         for k in range(col_blocks):
@@ -199,8 +222,10 @@
 
     def add_part(d):
         high = high_behind(d)
-        slot = part_in.at[high]
-        move(sem_z, d - 1, slot, slot, col=high * 2 + my_low).wait_recv()
+        for p, some in enumerate(pieces):
+            slot = part_in.at[high, some]
+            index = (d - 1) * count_pieces + p
+            move(sem_z, index, slot, slot, col=high * 2 + my_low).wait_recv()
         own[...] += part_in[high].astype(F32)
 
     load_w.wait()
@@ -213,9 +238,13 @@
     up[my_col] = (og_ref[...].astype(F32) * slope).astype(BF16)
 
     def up_high(d):
-        move(sem_u, d - 1, up.at[my_col], up.at[my_col], col=high_ahead(d) * 2 + my_low).start()
-
-    move(sem_f, 0, up.at[my_col], up.at[my_col], col=mate).start()
+        for p, some in enumerate(pieces):
+            mine = up.at[my_col, some]
+            index = (d - 1) * count_pieces + p
+            move(sem_u, index, mine, mine, col=high_ahead(d) * 2 + my_low).start()
+
+    for p, some in enumerate(pieces):
+        move(sem_f, p, up.at[my_col, some], up.at[my_col, some], col=mate).start()
     repeat(others, up_high)
     out_ref[...] = jnp.where(pre > 0, pre, decay - 1.0).astype(BF16)
 
@@ -236,15 +265,17 @@
 
     def back_high(d):
         source = high_behind(d) * 2 + my_low
-        slot = up.at[source]
-        move(sem_u, d - 1, slot, slot, col=source).wait_recv()
-        move(sem_f, d, slot, slot, col=mate).start()
+        for p, some in enumerate(pieces):
+            slot = up.at[source, some]
+            move(sem_u, (d - 1) * count_pieces + p, slot, slot, col=source).wait_recv()
+            move(sem_f, d * count_pieces + p, slot, slot, col=mate).start()
         back(source)
 
     def back_mate(d):
         source = high_behind(d) * 2 + 1 - my_low
-        slot = up.at[source]
-        move(sem_f, d, slot, slot, col=mate).wait_recv()
+        for p, some in enumerate(pieces):
+            slot = up.at[source, some]
+            move(sem_f, d * count_pieces + p, slot, slot, col=mate).wait_recv()
         back(source)
 
     back_mate(0)
@@ -333,12 +364,19 @@
             send("col", sem_w2, d, small, w2_in.at[my_col]).wait_send()
 
     def mate_sent(d):
-        move(sem_y, d, mate_part.at[0], mate_in.at[0], col=mate).wait_send()
-        move(sem_f, d, up.at[my_col], up.at[my_col], col=mate).wait_send()
+        for p, some in enumerate(pieces):
+            mine = up.at[my_col, some]
+            gone = mate_part.at[0, some]
+            move(sem_y, d * count_pieces + p, gone, mate_in.at[0, some], col=mate).wait_send()
+            move(sem_f, d * count_pieces + p, mine, mine, col=mate).wait_send()
 
     def high_sent(d):
-        move(sem_z, d - 1, part.at[0], part_in.at[0], col=mate).wait_send()
-        move(sem_u, d - 1, up.at[my_col], up.at[my_col], col=mate).wait_send()
+        for p, some in enumerate(pieces):
+            mine = up.at[my_col, some]
+            gone = part.at[0, some]
+            index = (d - 1) * count_pieces + p
+            move(sem_z, index, gone, part_in.at[0, some], col=mate).wait_send()
+            move(sem_u, index, mine, mine, col=mate).wait_send()
 
     repeat(list(range(half)), mate_sent)
     repeat(list(range(1, half)), high_sent)
@@ -375,7 +413,6 @@
     inside = pl.BlockSpec(memory_space=pltpu.VMEM)
     half = cols // 2
     assert cols == 2 * half
-    smem = pl.BlockSpec(memory_space=pltpu.SMEM)
     dma = pltpu.SemaphoreType.DMA
     shapes = (
         jax.ShapeDtypeStruct((nodes, width), BF16),
@@ -389,9 +426,11 @@
             pltpu.VMEM((nodes, width), BF16),
             pltpu.VMEM((width, width), F32),
         ),
-        in_specs=[smem, smem, place, place, place, place],
+        in_specs=[place, place, place, place, place, place],
         out_specs=(inside, inside, inside),
         scratch_shapes=[
+            pltpu.SMEM((slots,), jnp.int32),
+            pltpu.SMEM((1, 1), jnp.int32),
             pltpu.VMEM((slots + 1, block, block), BF16),
             pltpu.VMEM((width, width), BF16),
             pltpu.VMEM((nodes, width), BF16),
@@ -415,10 +454,10 @@
             pltpu.VMEM((rows, share, width), BF16),
             dma((7,)),
             dma((2, rows - 1)),
-            dma((2, half)),
-            dma((2, half - 1)),
-            dma((2, half - 1)),
-            dma((2, half)),
+            dma((2, half * 2)),
+            dma((2, (half - 1) * 2)),
+            dma((2, (half - 1) * 2)),
+            dma((2, half * 2)),
             dma((2, rows - 1)),
             dma((2, rows - 1)),
             dma((2, cols - 1)),

time: 41.4 us -> 40.2 us (0.971)
  Pallas kernels: 39.9 us -> 38.7 us
    pallas_call x1, Pallas kernels: 39.1 us -> 38 us  [body(): pl.pallas_call(functools.partial(kernel, rows, cols), out_shape=(pltpu.VM...]
where the time goes in v4:
time: 40.2 us; the launch traced here: 40 us
  Pallas kernels  38.7 us (96%)
  between operations  1.29 us (3%)
    pallas_call x1, Pallas kernels, body(): pl.pallas_call(functools.partial(kernel, rows, cols), out_shape=(pltpu.VM...  38 us

profile of v4, /device:TPU:0, one launch (start us, length us, event | category | flops | bytes accessed | tf_op | source)
XLA Modules:
  0.0 40.0 jit_solution(7218036752408726701)
XLA Ops:
  1.3 38.0 %shard_map.85 = (bf16[128,256]{1,0:T(8,128)(2,1)S(1)}, bf16[128,256]{1,0:T(8,128)(2,1)S(1)}, f32[256,256]{1,0:T(8,128)S(1)}) custom-call(s32[24]{0:T(128)} %bitcast.3, s32[1,1]{1,0:T(1,128)S(6)} %copy.9.count_hbm, bf16[128,256]{1,0:T(8,128)(2,1)} %x_hbm.1, bf16[256,256]{1,0:T(8,128)(2,1)} %w_hbm.1, bf16[128,256]{1,0:T(8,128)(2,1)} %og_hbm.1, ...), custom_call_target="tpu_custom_call" | custom-call | tf_op jit(solution)/shard_map/pallas_call | solution.py:422
  39.3 0.8 %shard_map.86 = (bf16[128,256]{1,0:T(8,128)(2,1)}, bf16[128,256]{1,0:T(8,128)(2,1)}, f32[256,256]{1,0:T(8,128)}) custom-call(bf16[128,256]{1,0:T(8,128)(2,1)S(1)} %get-tuple-element.6.out_ref, bf16[128,256]{1,0:T(8,128)(2,1)S(1)} %get-tuple-element.7.ig_ref, f32[256,256]{1,0:T(8,128)S(1)} %get-tuple-element.8.wg_ref), custom_call_target="tpu_custom_call" | custom-call | tf_op jit(solution)/shard_map/pallas_call | solution.py:476
